TPU v7x, 32 devices: a whole 2x2x4 slice. The times are simulated.
32 devices in a mesh: dp: 1, ctx: 32 (over z, y, x, core).
Axes of the slice: x: 2, y: 2, z: 4, core: 2. Of those that a mesh axis runs over, the one named last changes fastest.
Arguments:
- queries: bfloat16 [4096, 8192], P(('dp', 'ctx')), may hold values from -16 to 16
- out_grad: bfloat16 [4096, 8192], P(('dp', 'ctx')), may hold values from -6 to 6
- enc_states: bfloat16 [384, 1024], P(('dp', 'ctx')), may hold values from -8 to 8
- w_key: bfloat16 [1024, 8192], P('dp', 'ctx'), may hold values from -1 to 1
- w_value: bfloat16 [1024, 8192], P('dp', 'ctx'), may hold values from -0.1875 to 0.1875
- dec_segments: int32 [4096], P(('dp', 'ctx')), may hold values from 0 to 3, as said below
- enc_segments: int32 [384], P(('dp', 'ctx')), may hold values from 0 to 3, as said below
Outputs:
- query_grad: bfloat16 [4096, 8192], P(('dp', 'ctx'))
- enc_grad: bfloat16 [384, 1024], P(('dp', 'ctx'))
- w_key_grad: float32 [1024, 8192], P('dp', 'ctx')
- w_value_grad: float32 [1024, 8192], P('dp', 'ctx')
Inputs may be any that keep to these rules, and one draw needn't show every extreme that they name: `dec_segments`: within each pack the ids never fall along the tokens, and each of the 4 ids has one or more decoder tokens in the pack. `enc_segments`: within each pack the ids never fall along the tokens, and each of the 4 ids has two or more encoder tokens in the pack.
All inputs are finite; a program needn't handle non-finite values.
Results may differ from a plain program's by a relative error of at most 0.019.
Values may be sent and summed in bfloat16 or wider, within the bound.
A program may use at most 64 MiB of HBM per device.

v0:
```python
import math
import jax
import jax.numpy as jnp
from jax import lax
from jax.sharding import PartitionSpec as P

HEAD_DIM = 128


def attend(queries, out_grads, key_rows, value_rows, query_ids, key_ids):
    length, full_width = queries.shape
    key_count = key_rows.shape[0]
    head_count = full_width // HEAD_DIM
    group_size = min(head_count, 16)
    column_count = group_size * HEAD_DIM
    row_count = math.gcd(length, 1024)

    def head_group(number):
        column_start = number * column_count
        key_block = key_rows.reshape(key_count, group_size, HEAD_DIM)
        value_block = value_rows.reshape(key_count, group_size, HEAD_DIM)

        def query_block(totals, block_number):
            first_row = block_number * row_count
            query_part = lax.dynamic_slice(
                queries, (first_row, column_start), (row_count, column_count)
            ).reshape(row_count, group_size, HEAD_DIM)
            grad_part = lax.dynamic_slice(
                out_grads, (first_row, column_start), (row_count, column_count)
            ).reshape(row_count, group_size, HEAD_DIM)
            block_ids = lax.dynamic_slice_in_dim(query_ids, first_row, row_count, 0)
            allowed = block_ids[:, None] == key_ids[None, :]
            scores = jnp.einsum(
                "qhd,khd->hqk", query_part, key_block, preferred_element_type=jnp.float32
            )
            scores = jnp.where(allowed[None], scores, -jnp.inf)
            highest = jnp.max(scores, axis=2, keepdims=True)
            weights = jnp.exp(scores - highest)
            probability = weights / jnp.sum(weights, axis=2, keepdims=True)
            upstream = jnp.einsum(
                "qhd,khd->hqk", grad_part, value_block, preferred_element_type=jnp.float32
            )
            row_dot = jnp.sum(probability * upstream, axis=2, keepdims=True)
            score_grad = (probability * (upstream - row_dot)).astype(jnp.bfloat16)
            rounded = probability.astype(jnp.bfloat16)
            key_total = totals[0] + jnp.einsum(
                "hqk,qhd->khd", score_grad, query_part, preferred_element_type=jnp.float32
            )
            value_total = totals[1] + jnp.einsum(
                "hqk,qhd->khd", rounded, grad_part, preferred_element_type=jnp.float32
            )
            totals = (key_total, value_total)
            query_grad = jnp.einsum(
                "hqk,khd->qhd", score_grad, key_block, preferred_element_type=jnp.float32
            ).astype(jnp.bfloat16)
            return (totals, query_grad.reshape(row_count, column_count))

        zeros = jnp.zeros((key_count, group_size, HEAD_DIM), jnp.float32)
        totals, query_grads = lax.scan(
            query_block, (zeros, zeros), jnp.arange(length // row_count, dtype=jnp.int32)
        )
        results = ()
        results = results + (query_grads.reshape(length, column_count),)
        results = results + (
            totals[0].reshape(key_count, column_count),
            totals[1].reshape(key_count, column_count),
        )
        return results

    pieces = lax.map(head_group, jnp.arange(head_count // group_size, dtype=jnp.int32))
    return tuple(
        (jnp.moveaxis(piece, 0, 1).reshape(piece.shape[1], full_width) for piece in pieces)
    )


def body(queries, out_grad, enc_states, w_key, w_value, dec_segments, enc_segments):
    encoder, key_ids = (
        lax.all_gather(enc_states, "ctx", axis=0, tiled=True),
        lax.all_gather(enc_segments, "ctx", axis=0, tiled=True),
    )
    key_weight, value_weight = (
        lax.all_gather(w_key, "dp", axis=0, tiled=True),
        lax.all_gather(w_value, "dp", axis=0, tiled=True),
    )
    key_part = jnp.dot(encoder, key_weight, preferred_element_type=jnp.float32).astype(jnp.bfloat16)
    value_part = jnp.dot(encoder, value_weight, preferred_element_type=jnp.float32).astype(
        jnp.bfloat16
    )
    local_queries, local_grads = (
        lax.all_to_all(queries, "ctx", split_axis=1, concat_axis=0, tiled=True),
        lax.all_to_all(out_grad, "ctx", split_axis=1, concat_axis=0, tiled=True),
    )
    query_ids = lax.all_gather(dec_segments, "ctx", axis=0, tiled=True)
    head_grad, key_grad, value_grad = attend(
        local_queries, local_grads, key_part, value_part, query_ids, key_ids
    )
    query_grad = lax.all_to_all(head_grad, "ctx", split_axis=0, concat_axis=1, tiled=True)
    key_round = key_grad.astype(jnp.bfloat16)
    value_round = value_grad.astype(jnp.bfloat16)
    across = (((1,), (1,)), ((), ()))
    partial_value = lax.dot_general(
        key_round, key_weight, across, preferred_element_type=jnp.float32
    )
    partial_value = partial_value + lax.dot_general(
        value_round, value_weight, across, preferred_element_type=jnp.float32
    )
    enc_grad = lax.psum_scatter(
        partial_value.astype(jnp.bfloat16), "ctx", scatter_dimension=0, tiled=True
    )
    down = (((0,), (0,)), ((), ()))
    key_term = lax.dot_general(encoder, key_round, down, preferred_element_type=jnp.float32)
    value_term = lax.dot_general(encoder, value_round, down, preferred_element_type=jnp.float32)
    w_key_grad, w_value_grad = (
        lax.psum_scatter(
            key_term.astype(jnp.bfloat16), "dp", scatter_dimension=0, tiled=True
        ).astype(jnp.float32),
        lax.psum_scatter(
            value_term.astype(jnp.bfloat16), "dp", scatter_dimension=0, tiled=True
        ).astype(jnp.float32),
    )
    return (query_grad, enc_grad, w_key_grad, w_value_grad)


def solution(mesh):
    in_specs = (
        P(("dp", "ctx"), None),
        P(("dp", "ctx"), None),
        P(("dp", "ctx"), None),
        P("dp", "ctx"),
        P("dp", "ctx"),
        P(("dp", "ctx")),
        P(("dp", "ctx")),
    )
    out_specs = (P(("dp", "ctx"), None), P(("dp", "ctx"), None), P("dp", "ctx"), P("dp", "ctx"))
    return jax.shard_map(body, mesh=mesh, in_specs=in_specs, out_specs=out_specs, check_vma=False)
```

profile of v0, /device:TPU:3, one launch (start us, length us, event | category | flops | bytes accessed | tf_op | source)
XLA Modules:
  0.0 431.3 jit_solution(11465788982890251709)
XLA Ops:
  0.6 4.1 copy.68
  4.8 6.5 %all-to-all-start = ((bf16[128,32,256]{0,2,1:T(8,128)(2,1)}), bf16[128,32,256]{0,2,1:T(8,128)(2,1)}, u32[]{:S(2)}, u32[]{:S(2)}) async-start(bf16[128,32,256]{0,2,1:T(8,128)(2,1)} %bitcast.97), calls=%async_computation | async-start | bytes 4194304 | tf_op jit(solution)/shard_map/all_to_all | solution.py:90
  11.2 4.1 copy.70
  15.4 43.9 %all-to-all-done = bf16[128,32,256]{0,2,1:T(8,128)(2,1)} async-done(((bf16[128,32,256]{0,2,1:T(8,128)(2,1)}), bf16[128,32,256]{0,2,1:T(8,128)(2,1)}, u32[]{:S(2)}, u32[]{:S(2)}) %all-to-all-start) | async-done | bytes 2097184 | tf_op jit(solution)/shard_map/all_to_all | solution.py:90
  59.3 4.9 %all-to-all-start.1 = ((bf16[128,32,256]{0,2,1:T(8,128)(2,1)}), bf16[128,32,256]{0,2,1:T(8,128)(2,1)}, u32[]{:S(2)}, u32[]{:S(2)}) async-start(bf16[128,32,256]{0,2,1:T(8,128)(2,1)} %bitcast.96), calls=%async_computation.1 | async-start | bytes 4194304 | tf_op jit(solution)/shard_map/all_to_all | solution.py:91
  64.2 72.7 %all-gather.1 = bf16[32,12,1024]{2,1,0:T(8,128)(2,1)S(1)} all-gather(bf16[1,12,1024]{2,1,0:T(8,128)(2,1)S(1)} %bitcast.107), channel_id=1, replica_groups=mesh['dp'=1,'ctx'=32] {'ctx'}, dimensions={0}, use_global_device_ids=true | all-gather | bytes 811008 | tf_op jit(solution)/shard_map/all_gather | solution.py:78
  137.6 0.8 copy.74
  138.6 41.9 %all-reduce = s32[384]{0:T(512)S(1)} all-reduce(s32[384]{0:T(512)S(1)} %dynamic-update-slice), channel_id=1, replica_groups=mesh['dp'=1,'ctx'=32] {'ctx'}, use_global_device_ids=true, to_apply=%add | all-reduce | flops 384 | bytes 3072
  180.6 37.8 %all-gather = s32[32,1,128]{2,1,0:T(1,128)S(1)} all-gather(s32[1,1,128]{2,1,0:T(1,128)S(1)} %bitcast.108), channel_id=1, replica_groups=mesh['dp'=1,'ctx'=32] {'ctx'}, dimensions={0}, use_global_device_ids=true | all-gather | bytes 16896 | tf_op jit(solution)/shard_map/all_gather | solution.py:93
  218.8 4.1 copy.69
  222.9 4.1 copy.71
  227.0 57.9 %while.27 = (s32[]{:T(128)}, f32[384,2,128]{0,2,1:T(8,128)S(1)}, f32[384,2,128]{0,2,1:T(8,128)}, bf16[4,1024,256]{2,1,0:T(8,128)(2,1)}, s32[4]{0:T(128)S(1)}, /*...) while((s32[]{:T(128)}, f32[384,2,128]{0,2,1:T(8,128)S(1)}, ...), condition=%wide.region_4.5_spmd.clone, body=%wide.region_0.4_spmd.clone.sunk | while | flops 1017117056 | bytes 52033364 | solution.py:59
  227.0 0.6 dynamic_slice.32
  228.3 1.0 broadcast_compare_fusion.2
  229.3 1.3 constant_dynamic-slice_fusion.4
  231.0 4.0 fusion.71
  235.0 2.7 fusion.73
  237.8 0.6 multiply_reduce_fusion.2
  238.6 0.8 multiply_convert_fusion.2
  239.3 0.6 fusion.72
  240.7 0.8 constant_dynamic-update-slice_fusion.2
  241.5 0.6 dynamic_slice.32
  242.7 1.0 broadcast_compare_fusion.2
  243.8 1.3 constant_dynamic-slice_fusion.4
  245.5 3.9 fusion.71
  249.4 2.7 fusion.73
  252.3 0.6 multiply_reduce_fusion.2
  253.0 0.8 multiply_convert_fusion.2
  253.8 0.6 fusion.72
  255.1 0.8 constant_dynamic-update-slice_fusion.2
  257.2 1.0 broadcast_compare_fusion.2
  258.3 1.3 constant_dynamic-slice_fusion.4
  260.0 4.0 fusion.71
  263.9 2.7 fusion.73
  266.8 0.6 multiply_reduce_fusion.2
  267.5 0.8 multiply_convert_fusion.2
  268.3 0.6 fusion.72
  269.6 0.8 constant_dynamic-update-slice_fusion.2
  270.4 0.6 dynamic_slice.32
  271.7 1.0 broadcast_compare_fusion.2
  272.7 1.3 constant_dynamic-slice_fusion.4
  274.4 4.0 fusion.71
  278.4 2.7 fusion.73
  281.2 0.6 multiply_reduce_fusion.2
  282.0 0.8 multiply_convert_fusion.2
  282.8 0.6 fusion.72
  284.1 0.8 constant_dynamic-update-slice_fusion.2
  284.9 7.4 %all-to-all-start.2 = ((bf16[32,128,256]{2,1,0:T(8,128)(2,1)}), bf16[32,128,256]{2,1,0:T(8,128)(2,1)}, u32[]{:S(2)}, u32[]{:S(2)}) async-start(bf16[32,128,256]{2,1,0:T(8,128)(2,1)} %bitcast.100), calls=%async_computation.2 | async-start | bytes 4194304 | tf_op jit(solution)/shard_map/all_to_all | solution.py:97
  293.8 94.7 %fusion = bf16[16,1024]{1,0:T(8,128)(2,1)S(1)} fusion(bf16[384,1024]{1,0:T(8,128)(2,1)S(1)} %add_convert_fusion), kind=kCustom, calls=%all-reduce-scatter | all-reduce-scatter fusion | flops 524289 | bytes 819200
  388.5 1.3 collective-permute-start.6
  389.8 8.5 %collective-permute-start.5 = (bf16[16,1024]{1,0:T(8,128)(2,1)S(1)}, bf16[16,1024]{1,0:T(8,128)(2,1)S(1)}, u32[]{:S(2)}, u32[]{:S(2)}) collective-permute-start(bf16[16,1024]{1,0:T(8,128)(2,1)S(1)} %fusion), channel_id=1, source_target_pairs={{0,6},{1,7},{2,8},{3,9},{4,10},{5,11},{6,12},{7,13},{8,14},{9,15},... | collective-permute-start | bytes 98312
  398.3 1.3 collective-permute-start.7
  400.1 2.8 collective-permute-start.4
  402.9 1.3 collective-permute-start.3
  404.2 5.9 %collective-permute-start.2 = (bf16[16,1024]{1,0:T(8,128)(2,1)S(1)}, bf16[16,1024]{1,0:T(8,128)(2,1)S(1)}, u32[]{:S(2)}, u32[]{:S(2)}) collective-permute-start(bf16[16,1024]{1,0:T(8,128)(2,1)S(1)} %fusion), channel_id=1, source_target_pairs={{0,3},{1,4},{2,5},{3,6},{4,7},{5,8},{6,9},{7,10},{8,11},{9,12},{10... | collective-permute-start | bytes 98312
  410.2 2.5 collective-permute-start.1
  412.7 4.5 %collective-permute-start = (bf16[16,1024]{1,0:T(8,128)(2,1)S(1)}, bf16[16,1024]{1,0:T(8,128)(2,1)S(1)}, u32[]{:S(2)}, u32[]{:S(2)}) collective-permute-start(bf16[16,1024]{1,0:T(8,128)(2,1)S(1)} %fusion), channel_id=1, source_target_pairs={{0,1},{1,2},{2,3},{3,4},{4,5},{5,6},{6,7},{7,8},{8,9},{9,10},{10,1... | collective-permute-start | bytes 98312
  417.3 1.4 fusion.20
  418.7 1.3 copy.79
  420.0 1.3 copy.78
  421.4 1.2 concatenate
  422.5 0.6 constant_dynamic-slice_fusion.2
  423.2 4.1 copy.76
  427.2 4.1 copy.77
  (94 shorter events, 9.2 us)
Async XLA Ops:
  0.6 217.7 %copy-start = (bf16[1024,256]{1,0:T(8,128)(2,1)S(1)}, bf16[1024,256]{1,0:T(8,128)(2,1)}, u32[]{:S(2)}) copy-start(bf16[1024,256]{1,0:T(8,128)(2,1)} %param.12) | copy-start | bytes 1572868
  4.8 54.5 %all-to-all-start = ((bf16[128,32,256]{0,2,1:T(8,128)(2,1)}), bf16[128,32,256]{0,2,1:T(8,128)(2,1)}, u32[]{:S(2)}, u32[]{:S(2)}) async-start(bf16[128,32,256]{0,2,1:T(8,128)(2,1)} %bitcast.97), calls=%async_computation | async-start | bytes 4194304 | tf_op jit(solution)/shard_map/all_to_all | solution.py:90
  59.3 5.0 %copy-start.9 = (bf16[12,1024]{1,0:T(8,128)(2,1)S(1)}, bf16[12,1024]{1,0:T(8,128)(2,1)}, u32[]{:S(2)}) copy-start(bf16[12,1024]{1,0:T(8,128)(2,1)} %param.11) | copy-start | bytes 73732
  59.3 163.7 %all-to-all-start.1 = ((bf16[128,32,256]{0,2,1:T(8,128)(2,1)}), bf16[128,32,256]{0,2,1:T(8,128)(2,1)}, u32[]{:S(2)}, u32[]{:S(2)}) async-start(bf16[128,32,256]{0,2,1:T(8,128)(2,1)} %bitcast.96), calls=%async_computation.1 | async-start | bytes 4194304 | tf_op jit(solution)/shard_map/all_to_all | solution.py:91
  64.2 72.9 %copy-start.3 = (bf16[1024,256]{1,0:T(8,128)(2,1)S(1)}, bf16[1024,256]{1,0:T(8,128)(2,1)}, u32[]{:S(2)}) copy-start(bf16[1024,256]{1,0:T(8,128)(2,1)} %param.13) | copy-start | bytes 1572868
  136.9 1.5 copy-start.11
  136.9 43.6 %copy-start.10 = (s32[128]{0:T(128)S(1)}, s32[128]{0:T(128)}, u32[]{:S(2)}) copy-start(s32[128]{0:T(128)} %param.14) | copy-start | bytes 1540
  231.0 4.0 copy-start.5
  235.0 2.8 copy-start.1
  235.0 2.8 copy-start.8
  237.8 0.7 copy-start.6
  245.5 4.0 copy-start.5
  249.4 2.8 copy-start.1
  249.4 2.8 copy-start.8
  252.3 0.7 copy-start.6
  260.0 4.0 copy-start.5
  263.9 2.8 copy-start.1
  263.9 2.8 copy-start.8
  266.8 0.7 copy-start.6
  274.4 4.0 copy-start.5
  278.4 2.8 copy-start.1
  278.4 2.8 copy-start.8
  281.2 0.7 copy-start.6
  284.9 7.5 %copy-start.7 = (f32[384,2,128]{0,2,1:T(8,128)S(1)}, f32[384,2,128]{0,2,1:T(8,128)}, u32[]{:S(2)}) copy-start(f32[384,2,128]{0,2,1:T(8,128)} %get-tuple-element.121) | copy-start | bytes 1179652
  284.9 138.3 %all-to-all-start.2 = ((bf16[32,128,256]{2,1,0:T(8,128)(2,1)}), bf16[32,128,256]{2,1,0:T(8,128)(2,1)}, u32[]{:S(2)}, u32[]{:S(2)}) async-start(bf16[32,128,256]{2,1,0:T(8,128)(2,1)} %bitcast.100), calls=%async_computation.2 | async-start | bytes 4194304 | tf_op jit(solution)/shard_map/all_to_all | solution.py:97
  292.3 1.0 copy-start.4
  388.5 21.6 %collective-permute-start.6 = (bf16[16,1024]{1,0:T(8,128)(2,1)S(1)}, bf16[16,1024]{1,0:T(8,128)(2,1)S(1)}, u32[]{:S(2)}, u32[]{:S(2)}) collective-permute-start(bf16[16,1024]{1,0:T(8,128)(2,1)S(1)} %fusion), channel_id=1, source_target_pairs={{0,7},{1,8},{2,9},{3,10},{4,11},{5,12},{6,13},{7,14},{8,15},{9,16}... | collective-permute-start | bytes 98312
  389.8 22.9 %collective-permute-start.5 = (bf16[16,1024]{1,0:T(8,128)(2,1)S(1)}, bf16[16,1024]{1,0:T(8,128)(2,1)S(1)}, u32[]{:S(2)}, u32[]{:S(2)}) collective-permute-start(bf16[16,1024]{1,0:T(8,128)(2,1)S(1)} %fusion), channel_id=1, source_target_pairs={{0,6},{1,7},{2,8},{3,9},{4,10},{5,11},{6,12},{7,13},{8,14},{9,15},... | collective-permute-start | bytes 98312
  398.3 5.9 %collective-permute-start.7 = (bf16[12,1024]{1,0:T(8,128)(2,1)S(1)}, bf16[12,1024]{1,0:T(8,128)(2,1)S(1)}, u32[]{:S(2)}, u32[]{:S(2)}) collective-permute-start(bf16[12,1024]{1,0:T(8,128)(2,1)S(1)} %slice), channel_id=1, source_target_pairs={{0,8},{1,9},{2,10},{3,11},{4,12},{5,13},{6,14},{7,15},{8,16},{9,17... | collective-permute-start | bytes 73736
  400.1 21.3 %collective-permute-start.4 = (bf16[16,1024]{1,0:T(8,128)(2,1)S(1)}, bf16[16,1024]{1,0:T(8,128)(2,1)S(1)}, u32[]{:S(2)}, u32[]{:S(2)}) collective-permute-start(bf16[16,1024]{1,0:T(8,128)(2,1)S(1)} %fusion), channel_id=1, source_target_pairs={{0,5},{1,6},{2,7},{3,8},{4,9},{5,10},{6,11},{7,12},{8,13},{9,14},{... | collective-permute-start | bytes 98312
  402.9 18.4 %collective-permute-start.3 = (bf16[16,1024]{1,0:T(8,128)(2,1)S(1)}, bf16[16,1024]{1,0:T(8,128)(2,1)S(1)}, u32[]{:S(2)}, u32[]{:S(2)}) collective-permute-start(bf16[16,1024]{1,0:T(8,128)(2,1)S(1)} %fusion), channel_id=1, source_target_pairs={{0,4},{1,5},{2,6},{3,7},{4,8},{5,9},{6,10},{7,11},{8,12},{9,13},{1... | collective-permute-start | bytes 98312
  404.2 17.1 %collective-permute-start.2 = (bf16[16,1024]{1,0:T(8,128)(2,1)S(1)}, bf16[16,1024]{1,0:T(8,128)(2,1)S(1)}, u32[]{:S(2)}, u32[]{:S(2)}) collective-permute-start(bf16[16,1024]{1,0:T(8,128)(2,1)S(1)} %fusion), channel_id=1, source_target_pairs={{0,3},{1,4},{2,5},{3,6},{4,7},{5,8},{6,9},{7,10},{8,11},{9,12},{10... | collective-permute-start | bytes 98312
  410.2 11.2 %collective-permute-start.1 = (bf16[16,1024]{1,0:T(8,128)(2,1)S(1)}, bf16[16,1024]{1,0:T(8,128)(2,1)S(1)}, u32[]{:S(2)}, u32[]{:S(2)}) collective-permute-start(bf16[16,1024]{1,0:T(8,128)(2,1)S(1)} %fusion), channel_id=1, source_target_pairs={{0,2},{1,3},{2,4},{3,5},{4,6},{5,7},{6,8},{7,9},{8,10},{9,11},{10,... | collective-permute-start | bytes 98312
  412.7 8.6 %collective-permute-start = (bf16[16,1024]{1,0:T(8,128)(2,1)S(1)}, bf16[16,1024]{1,0:T(8,128)(2,1)S(1)}, u32[]{:S(2)}, u32[]{:S(2)}) collective-permute-start(bf16[16,1024]{1,0:T(8,128)(2,1)S(1)} %fusion), channel_id=1, source_target_pairs={{0,1},{1,2},{2,3},{3,4},{4,5},{5,6},{6,7},{7,8},{8,9},{9,10},{10,1... | collective-permute-start | bytes 98312
  418.7 1.3 copy-start.2
where the time goes:
time: 433 us; the launch traced here: 431 us
  blocking collectives  247 us (57%)
  starting transfers between devices  47 us (11%)
  local copies, waits for them, and re-layouts  45 us (10%)
  waiting for transfers between devices  43.9 us (10%)
  matrix products  37 us (9%)
  other arithmetic  7.34 us (2%)
    unnamed x2, blocking collectives  137 us
    all_gather x1, blocking collectives, body(): lax.all_gather(enc_states, 'ctx', axis=0, tiled=True)  72.7 us
    all_to_all x1, waiting for transfers between devices, body(): lax.all_to_all(queries, 'ctx', split_axis=1, concat_axis=0, tiled=True)  43.9 us
    all_gather x1, blocking collectives, body(): query_ids = lax.all_gather(dec_segments, 'ctx', axis=0, tiled=True)  37.8 us
    unnamed x8, starting transfers between devices  28.2 us
    unnamed x28, local copies, waits for them, and re-layouts  18.5 us
    sub x4, matrix products, query_block(): weights = jnp.exp(scores - highest)  15.8 us
    dot_general x4, matrix products, query_block(): jnp.einsum('hqk,qhd->khd', rounded, grad_part, preferred_element_type=jnp...  10.9 us
  transfers between devices with their start and end apart: 11, of which 1 were waited for; matrix products, arithmetic and copies ran while one was open for 26% of the time, Pallas kernels for 0%

commit v1 on v0

--- a/solution.py
+++ b/solution.py
@@ -5,6 +5,13 @@
 from jax.sharding import PartitionSpec as P
 
 HEAD_DIM = 128
+
+
+def swap_blocks(x, mesh_axis, split, join):
+    count = lax.axis_size(mesh_axis)
+    blocks = jnp.stack(jnp.split(x, count, axis=split), axis=0)
+    blocks = lax.all_to_all(blocks, mesh_axis, split_axis=0, concat_axis=0)
+    return jnp.concatenate(blocks, axis=join)
 
 
 def attend(queries, out_grads, key_rows, value_rows, query_ids, key_ids):
@@ -87,7 +94,7 @@
         jnp.bfloat16
     )
     local_queries, local_grads = (
-        lax.all_to_all(queries, "ctx", split_axis=1, concat_axis=0, tiled=True),
+        swap_blocks(queries, "ctx", 1, 0),
         lax.all_to_all(out_grad, "ctx", split_axis=1, concat_axis=0, tiled=True),
     )
     query_ids = lax.all_gather(dec_segments, "ctx", axis=0, tiled=True)

time: 433 us -> 432 us (level)
  waiting for transfers between devices: 43.9 us -> 1.19 us
  local copies, waits for them, and re-layouts: 45 us -> 85.2 us
    all_to_all x1, waiting for transfers between devices: 43.9 us -> 0.01 us  [swap_blocks(): blocks = lax.all_to_all(blocks, mesh_axis, split_axis=0, concat_axis=0)]
    unnamed x28 -> x62, local copies, waits for them, and re-layouts: 18.5 us -> 62.1 us
  transfers between devices with their start and end apart: 11 -> 11, of which waited for: 1 -> 1; matrix products, arithmetic and copies ran while one was open for 26% -> 37% of each run, Pallas kernels for 0% -> 0%
where the time goes in v1:
time: 432 us; the launch traced here: 428 us
  blocking collectives  247 us (57%)
  local copies, waits for them, and re-layouts  85.2 us (20%)
  starting transfers between devices  47.1 us (11%)
  matrix products  36.1 us (8%)
  other arithmetic  7.34 us (2%)
    unnamed x2, blocking collectives  137 us
    all_gather x1, blocking collectives, body(): lax.all_gather(enc_states, 'ctx', axis=0, tiled=True)  72.7 us
    unnamed x62, local copies, waits for them, and re-layouts  62.1 us
    all_gather x1, blocking collectives, body(): query_ids = lax.all_gather(dec_segments, 'ctx', axis=0, tiled=True)  37.8 us
    unnamed x8, starting transfers between devices  28.4 us
    sub x4, matrix products, query_block(): weights = jnp.exp(scores - highest)  15.8 us
    dot_general x4, matrix products, query_block(): jnp.einsum('hqk,qhd->khd', rounded, grad_part, preferred_element_type=jnp...  10.9 us
  transfers between devices with their start and end apart: 11, of which 1 were waited for; matrix products, arithmetic and copies ran while one was open for 37% of the time, Pallas kernels for 0%

profile of v1, /device:TPU:3, one launch (start us, length us, event | category | flops | bytes accessed | tf_op | source)
XLA Modules:
  0.0 427.8 jit_solution(15906440587263924205)
XLA Ops:
  0.6 4.1 copy.68
  4.8 6.4 %all-to-all-start.1 = ((bf16[128,32,256]{0,2,1:T(8,128)(2,1)}), bf16[128,32,256]{0,2,1:T(8,128)(2,1)S(1)}, u32[]{:S(2)}, u32[]{:S(2)}) async-start(bf16[128,32,256]{0,2,1:T(8,128)(2,1)} %bitcast.156), calls=%async_computation.1 | async-start | bytes 4194304 | tf_op jit(solution)/shard_map/all_to_all | solution.py:98
  11.2 1.5 constant_dynamic-update-slice_fusion.32
  12.7 1.5 constant_dynamic-update-slice_fusion.31
  14.1 1.5 constant_dynamic-update-slice_fusion.30
  15.6 1.5 constant_dynamic-update-slice_fusion.29
  17.0 1.5 constant_dynamic-update-slice_fusion.28
  18.5 1.5 constant_dynamic-update-slice_fusion.27
  20.0 1.5 constant_dynamic-update-slice_fusion.26
  21.4 1.5 constant_dynamic-update-slice_fusion.25
  22.9 1.5 constant_dynamic-update-slice_fusion.24
  24.3 1.5 constant_dynamic-update-slice_fusion.23
  25.8 1.5 constant_dynamic-update-slice_fusion.22
  27.3 1.5 constant_dynamic-update-slice_fusion.21
  28.7 1.5 constant_dynamic-update-slice_fusion.20
  30.2 1.5 constant_dynamic-update-slice_fusion.19
  31.7 1.5 constant_dynamic-update-slice_fusion.18
  33.1 1.5 constant_dynamic-update-slice_fusion.17
  34.6 1.5 constant_dynamic-update-slice_fusion.16
  36.1 1.5 constant_dynamic-update-slice_fusion.15
  37.5 1.5 constant_dynamic-update-slice_fusion.14
  39.0 1.5 constant_dynamic-update-slice_fusion.13
  40.5 1.5 constant_dynamic-update-slice_fusion.12
  41.9 1.5 constant_dynamic-update-slice_fusion.11
  43.4 1.5 constant_dynamic-update-slice_fusion.10
  44.8 1.5 constant_dynamic-update-slice_fusion.9
  46.3 1.5 constant_dynamic-update-slice_fusion.8
  47.8 1.5 constant_dynamic-update-slice_fusion.7
  49.2 1.5 constant_dynamic-update-slice_fusion.6
  50.7 1.5 constant_dynamic-update-slice_fusion.5
  52.2 1.5 constant_dynamic-update-slice_fusion.4
  53.6 1.5 constant_dynamic-update-slice_fusion.3
  55.1 1.5 constant_dynamic-update-slice_fusion.2
  56.5 1.5 constant_dynamic-update-slice_fusion.1
  59.2 4.9 %all-to-all-start = ((bf16[32,128,256]{2,1,0:T(8,128)(2,1)}), bf16[32,128,256]{2,1,0:T(8,128)(2,1)}, u32[]{:S(2)}, u32[]{:S(2)}) async-start(bf16[32,128,256]{2,1,0:T(8,128)(2,1)} %constant_dynamic-update-slice_fusion.1), calls=%async_computation | async-start | bytes 4194304 | tf_op jit(solution)/shard_map/all_to_all | solution.py:13
  64.1 72.7 %all-gather.1 = bf16[32,12,1024]{2,1,0:T(8,128)(2,1)S(1)} all-gather(bf16[1,12,1024]{2,1,0:T(8,128)(2,1)S(1)} %bitcast.166), channel_id=1, replica_groups=mesh['dp'=1,'ctx'=32] {'ctx'}, dimensions={0}, use_global_device_ids=true | all-gather | bytes 811008 | tf_op jit(solution)/shard_map/all_gather | solution.py:85
  138.5 41.9 %all-reduce = s32[384]{0:T(512)S(1)} all-reduce(s32[384]{0:T(512)S(1)} %dynamic-update-slice), channel_id=1, replica_groups=mesh['dp'=1,'ctx'=32] {'ctx'}, use_global_device_ids=true, to_apply=%add | all-reduce | flops 384 | bytes 3072
  180.5 37.8 %all-gather = s32[32,1,128]{2,1,0:T(1,128)S(1)} all-gather(s32[1,1,128]{2,1,0:T(1,128)S(1)} %bitcast.167), channel_id=1, replica_groups=mesh['dp'=1,'ctx'=32] {'ctx'}, dimensions={0}, use_global_device_ids=true | all-gather | bytes 16896 | tf_op jit(solution)/shard_map/all_gather | solution.py:100
  218.7 4.1 copy.69
  222.8 57.9 %while.27 = (s32[]{:T(128)}, f32[384,2,128]{0,2,1:T(8,128)S(1)}, f32[384,2,128]{0,2,1:T(8,128)}, bf16[4,1024,256]{2,1,0:T(8,128)(2,1)}, s32[4]{0:T(128)S(1)}, /*...) while((s32[]{:T(128)}, f32[384,2,128]{0,2,1:T(8,128)S(1)}, ...), condition=%wide.region_4.5_spmd.clone, body=%wide.region_0.4_spmd.clone.sunk | while | flops 1017117056 | bytes 52033364 | solution.py:66
  226.8 4.0 fusion.71
  230.8 2.7 fusion.73
  241.3 4.0 fusion.71
  245.3 2.7 fusion.73
  254.1 1.3 constant_dynamic-slice_fusion.4
  255.8 4.0 fusion.71
  259.7 2.7 fusion.73
  270.2 4.0 fusion.71
  274.2 2.7 fusion.73
  280.7 7.4 %all-to-all-start.2 = ((bf16[32,128,256]{2,1,0:T(8,128)(2,1)}), bf16[32,128,256]{2,1,0:T(8,128)(2,1)}, u32[]{:S(2)}, u32[]{:S(2)}) async-start(bf16[32,128,256]{2,1,0:T(8,128)(2,1)} %bitcast.159), calls=%async_computation.2 | async-start | bytes 4194304 | tf_op jit(solution)/shard_map/all_to_all | solution.py:104
  289.7 94.6 %fusion = bf16[16,1024]{1,0:T(8,128)(2,1)S(1)} fusion(bf16[384,1024]{1,0:T(8,128)(2,1)S(1)} %add_convert_fusion), kind=kCustom, calls=%all-reduce-scatter | all-reduce-scatter fusion | flops 524289 | bytes 819200
  384.4 1.4 collective-permute-start.6
  385.8 8.5 %collective-permute-start.5 = (bf16[16,1024]{1,0:T(8,128)(2,1)S(1)}, bf16[16,1024]{1,0:T(8,128)(2,1)S(1)}, u32[]{:S(2)}, u32[]{:S(2)}) collective-permute-start(bf16[16,1024]{1,0:T(8,128)(2,1)S(1)} %fusion), channel_id=1, source_target_pairs={{0,6},{1,7},{2,8},{3,9},{4,10},{5,11},{6,12},{7,13},{8,14},{9,15},... | collective-permute-start | bytes 98312
  394.3 1.3 collective-permute-start.7
  396.0 3.4 collective-permute-start.4
  399.5 1.9 collective-permute-start.3
  401.3 4.8 %collective-permute-start.2 = (bf16[16,1024]{1,0:T(8,128)(2,1)S(1)}, bf16[16,1024]{1,0:T(8,128)(2,1)}, u32[]{:S(2)}, u32[]{:S(2)}) collective-permute-start(bf16[16,1024]{1,0:T(8,128)(2,1)S(1)} %fusion), channel_id=1, source_target_pairs={{0,3},{1,4},{2,5},{3,6},{4,7},{5,8},{6,9},{7,10},{8,11},{9,12},{10... | collective-permute-start | bytes 98312
  406.1 2.5 collective-permute-start.1
  408.7 4.5 %collective-permute-start = (bf16[16,1024]{1,0:T(8,128)(2,1)S(1)}, bf16[16,1024]{1,0:T(8,128)(2,1)}, u32[]{:S(2)}, u32[]{:S(2)}) collective-permute-start(bf16[16,1024]{1,0:T(8,128)(2,1)S(1)} %fusion), channel_id=1, source_target_pairs={{0,1},{1,2},{2,3},{3,4},{4,5},{5,6},{6,7},{7,8},{8,9},{9,10},{10,1... | collective-permute-start | bytes 98312
  413.7 1.3 copy.76
  415.0 1.3 copy.75
  416.4 4.7 %concatenate = bf16[140,1024]{1,0:T(8,128)(2,1)S(1)} concatenate(bf16[12,1024]{1,0:T(8,128)(2,1)S(1)} %collective-permute-done.7, bf16[16,1024]{1,0:T(8,128)(2,1)S(1)} %collective-permute-done.6, bf16[16,1024]{1,0:T(8,128)(2,1)S(1)} %collective-permute-done.5, bf16[16,1024]{1,0:T(8,128)(2,1)} %collective-permute-done.4, bf16[16,1024]{1,0:T(8,128)(2,1)} %collective-permute-done.3, ...), dimensions={0} | concatenate | bytes 573440
  421.7 3.2 copy.73
  424.9 2.9 copy.74
  (128 shorter events, 33.4 us)
Async XLA Ops:
  0.6 217.6 %copy-start = (bf16[1024,256]{1,0:T(8,128)(2,1)S(1)}, bf16[1024,256]{1,0:T(8,128)(2,1)}, u32[]{:S(2)}) copy-start(bf16[1024,256]{1,0:T(8,128)(2,1)} %param.12) | copy-start | bytes 1572868
  4.8 54.4 %all-to-all-start.1 = ((bf16[128,32,256]{0,2,1:T(8,128)(2,1)}), bf16[128,32,256]{0,2,1:T(8,128)(2,1)S(1)}, u32[]{:S(2)}, u32[]{:S(2)}) async-start(bf16[128,32,256]{0,2,1:T(8,128)(2,1)} %bitcast.156), calls=%async_computation.1 | async-start | bytes 4194304 | tf_op jit(solution)/shard_map/all_to_all | solution.py:98
  58.0 6.1 %copy-start.11 = (bf16[12,1024]{1,0:T(8,128)(2,1)S(1)}, bf16[12,1024]{1,0:T(8,128)(2,1)}, u32[]{:S(2)}) copy-start(bf16[12,1024]{1,0:T(8,128)(2,1)} %param.11) | copy-start | bytes 73732
  59.2 4.9 %copy-start.2 = (bf16[128,32,256]{0,2,1:T(8,128)(2,1)}, bf16[128,32,256]{0,2,1:T(8,128)(2,1)S(1)}, u32[]{:S(2)}) copy-start(bf16[128,32,256]{0,2,1:T(8,128)(2,1)S(1)} %all-to-all-done.1) | copy-start | bytes 6291460
  59.2 163.6 %all-to-all-start = ((bf16[32,128,256]{2,1,0:T(8,128)(2,1)}), bf16[32,128,256]{2,1,0:T(8,128)(2,1)}, u32[]{:S(2)}, u32[]{:S(2)}) async-start(bf16[32,128,256]{2,1,0:T(8,128)(2,1)} %constant_dynamic-update-slice_fusion.1), calls=%async_computation | async-start | bytes 4194304 | tf_op jit(solution)/shard_map/all_to_all | solution.py:13
  64.1 72.9 %copy-start.3 = (bf16[1024,256]{1,0:T(8,128)(2,1)S(1)}, bf16[1024,256]{1,0:T(8,128)(2,1)}, u32[]{:S(2)}) copy-start(bf16[1024,256]{1,0:T(8,128)(2,1)} %param.13) | copy-start | bytes 1572868
  136.8 1.5 copy-start.13
  136.8 43.6 %copy-start.12 = (s32[128]{0:T(128)S(1)}, s32[128]{0:T(128)}, u32[]{:S(2)}) copy-start(s32[128]{0:T(128)} %param.14) | copy-start | bytes 1540
  226.8 4.0 copy-start.7
  230.8 2.8 copy-start.1
  230.8 2.8 copy-start.10
  233.6 0.7 copy-start.8
  241.3 4.0 copy-start.7
  245.2 2.8 copy-start.1
  245.3 2.8 copy-start.10
  248.1 0.7 copy-start.8
  255.8 4.0 copy-start.7
  259.7 2.8 copy-start.1
  259.7 2.8 copy-start.10
  262.6 0.7 copy-start.8
  270.2 4.0 copy-start.7
  274.2 2.8 copy-start.1
  274.2 2.8 copy-start.10
  277.0 0.7 copy-start.8
  280.7 7.5 %copy-start.9 = (f32[384,2,128]{0,2,1:T(8,128)S(1)}, f32[384,2,128]{0,2,1:T(8,128)}, u32[]{:S(2)}) copy-start(f32[384,2,128]{0,2,1:T(8,128)} %get-tuple-element.121) | copy-start | bytes 1179652
  280.7 141.0 %all-to-all-start.2 = ((bf16[32,128,256]{2,1,0:T(8,128)(2,1)}), bf16[32,128,256]{2,1,0:T(8,128)(2,1)}, u32[]{:S(2)}, u32[]{:S(2)}) async-start(bf16[32,128,256]{2,1,0:T(8,128)(2,1)} %bitcast.159), calls=%async_computation.2 | async-start | bytes 4194304 | tf_op jit(solution)/shard_map/all_to_all | solution.py:104
  288.2 1.1 copy-start.4
  288.2 0.7 copy-start.5
  384.3 28.9 %copy-start.6 = (bf16[384,2,128]{0,2,1:T(8,128)(2,1)S(1)}, bf16[384,2,128]{0,2,1:T(8,128)(2,1)}, u32[]{:S(2)}) copy-start(bf16[384,2,128]{0,2,1:T(8,128)(2,1)} %copy-done.5) | copy-start | bytes 589828
  384.4 21.8 %collective-permute-start.6 = (bf16[16,1024]{1,0:T(8,128)(2,1)S(1)}, bf16[16,1024]{1,0:T(8,128)(2,1)S(1)}, u32[]{:S(2)}, u32[]{:S(2)}) collective-permute-start(bf16[16,1024]{1,0:T(8,128)(2,1)S(1)} %fusion), channel_id=1, source_target_pairs={{0,7},{1,8},{2,9},{3,10},{4,11},{5,12},{6,13},{7,14},{8,15},{9,16}... | collective-permute-start | bytes 98312
  385.8 22.9 %collective-permute-start.5 = (bf16[16,1024]{1,0:T(8,128)(2,1)S(1)}, bf16[16,1024]{1,0:T(8,128)(2,1)S(1)}, u32[]{:S(2)}, u32[]{:S(2)}) collective-permute-start(bf16[16,1024]{1,0:T(8,128)(2,1)S(1)} %fusion), channel_id=1, source_target_pairs={{0,6},{1,7},{2,8},{3,9},{4,10},{5,11},{6,12},{7,13},{8,14},{9,15},... | collective-permute-start | bytes 98312
  394.3 7.1 %collective-permute-start.7 = (bf16[12,1024]{1,0:T(8,128)(2,1)S(1)}, bf16[12,1024]{1,0:T(8,128)(2,1)S(1)}, u32[]{:S(2)}, u32[]{:S(2)}) collective-permute-start(bf16[12,1024]{1,0:T(8,128)(2,1)S(1)} %slice), channel_id=1, source_target_pairs={{0,8},{1,9},{2,10},{3,11},{4,12},{5,13},{6,14},{7,15},{8,16},{9,17... | collective-permute-start | bytes 73736
  396.0 20.3 %collective-permute-start.4 = (bf16[16,1024]{1,0:T(8,128)(2,1)S(1)}, bf16[16,1024]{1,0:T(8,128)(2,1)}, u32[]{:S(2)}, u32[]{:S(2)}) collective-permute-start(bf16[16,1024]{1,0:T(8,128)(2,1)S(1)} %fusion), channel_id=1, source_target_pairs={{0,5},{1,6},{2,7},{3,8},{4,9},{5,10},{6,11},{7,12},{8,13},{9,14},{... | collective-permute-start | bytes 98312
  399.5 16.9 %collective-permute-start.3 = (bf16[16,1024]{1,0:T(8,128)(2,1)S(1)}, bf16[16,1024]{1,0:T(8,128)(2,1)}, u32[]{:S(2)}, u32[]{:S(2)}) collective-permute-start(bf16[16,1024]{1,0:T(8,128)(2,1)S(1)} %fusion), channel_id=1, source_target_pairs={{0,4},{1,5},{2,6},{3,7},{4,8},{5,9},{6,10},{7,11},{8,12},{9,13},{1... | collective-permute-start | bytes 98312
  401.3 15.0 %collective-permute-start.2 = (bf16[16,1024]{1,0:T(8,128)(2,1)S(1)}, bf16[16,1024]{1,0:T(8,128)(2,1)}, u32[]{:S(2)}, u32[]{:S(2)}) collective-permute-start(bf16[16,1024]{1,0:T(8,128)(2,1)S(1)} %fusion), channel_id=1, source_target_pairs={{0,3},{1,4},{2,5},{3,6},{4,7},{5,8},{6,9},{7,10},{8,11},{9,12},{10... | collective-permute-start | bytes 98312
  406.1 10.2 %collective-permute-start.1 = (bf16[16,1024]{1,0:T(8,128)(2,1)S(1)}, bf16[16,1024]{1,0:T(8,128)(2,1)}, u32[]{:S(2)}, u32[]{:S(2)}) collective-permute-start(bf16[16,1024]{1,0:T(8,128)(2,1)S(1)} %fusion), channel_id=1, source_target_pairs={{0,2},{1,3},{2,4},{3,5},{4,6},{5,7},{6,8},{7,9},{8,10},{9,11},{10,... | collective-permute-start | bytes 98312
  408.7 7.6 %collective-permute-start = (bf16[16,1024]{1,0:T(8,128)(2,1)S(1)}, bf16[16,1024]{1,0:T(8,128)(2,1)}, u32[]{:S(2)}, u32[]{:S(2)}) collective-permute-start(bf16[16,1024]{1,0:T(8,128)(2,1)S(1)} %fusion), channel_id=1, source_target_pairs={{0,1},{1,2},{2,3},{3,4},{4,5},{5,6},{6,7},{7,8},{8,9},{9,10},{10,1... | collective-permute-start | bytes 98312
